TPU v7x, 512 devices: a whole 4x8x8 slice. The times are simulated.
512 devices in a mesh: section: 64 (over z, y_hi, core), tensor: 8 (over x, y_lo).
Axes of the slice: x: 4, y: 8 (y_hi: 4, y_lo: 2; y = y_hi * 2 + y_lo), z: 8, core: 2. Of those that a mesh axis runs over, the one named last changes fastest.
Arguments:
- grad_in: bfloat16 [64, 256, 6144], P('section', None, 'tensor'), may hold values from -6 to 6
- loss_grad: bfloat16 [256, 6144], P(None, 'tensor'), may hold values from -6 to 6
- queries: bfloat16 [64, 2, 256, 6144], P('section', None, None, 'tensor'), may hold values from -32 to 32
- attn_keys: bfloat16 [64, 2, 256, 6144], P('section', None, None, 'tensor'), may hold values from -32 to 32
- stored_input: bfloat16 [64, 2, 256, 6144], P('section', None, 'tensor'), may hold values from -6 to 6
- block_scales: bfloat16 [64, 2, 256, 48], P('section', None, 'tensor'), may hold values from 0.25 to 4
Outputs:
- grad_next: bfloat16 [64, 256, 6144], P('section', None, 'tensor')
- query_grad: bfloat16 [64, 2, 256, 6144], P('section', None, None, 'tensor')
- key_grad: bfloat16 [64, 2, 256, 6144], P('section', None, None, 'tensor')
All inputs are finite; a program needn't handle non-finite values.
Results may differ from a plain program's by a relative error of at most 0.0063.
Values may be sent and summed in bfloat16 or wider, within the bound.
A program may use at most 64 MiB of HBM per device.

v0:
```python
import math
import jax
import jax.numpy as jnp
from jax import lax
from jax.sharding import PartitionSpec as P

HD = 128


def passed_along(value, axis, steps):
    count = lax.axis_size(axis)
    leading, last = (max(0, -steps), min(count, count - steps))
    return lax.ppermute(value, axis, [(source, source + steps) for source in range(leading, last)])


def to_heads(flat):
    tokens, width = flat.shape
    return flat.reshape(tokens, width // HD, HD).transpose(1, 0, 2)


def from_heads(split):
    heads, tokens, depth = split.shape
    return split.transpose(1, 0, 2).reshape(tokens, heads * depth)


def attention_weights(query_heads, key_heads):
    tokens = query_heads.shape[1]
    scores = jnp.einsum(
        "htd,hjd->htj", query_heads, key_heads, preferred_element_type=jnp.float32
    ) * (1.0 / math.sqrt(HD))
    causal = lax.broadcasted_iota(jnp.int32, (tokens, tokens), 0) >= lax.broadcasted_iota(
        jnp.int32, (tokens, tokens), 1
    )
    scores = jnp.where(causal[None], scores, -1e30)
    scores = scores - jnp.max(scores, axis=-1, keepdims=True)
    expon = jnp.exp(scores)
    return expon / jnp.sum(expon, axis=-1, keepdims=True)


def value_grad(weights, upstream, upstream_heads):
    rounded = weights.astype(jnp.bfloat16)
    carried = jnp.einsum(
        "htj,htd->hjd", rounded, upstream_heads, preferred_element_type=jnp.float32
    )
    return (upstream.astype(jnp.float32) + from_heads(carried)).astype(jnp.bfloat16)


def score_grads(weights, upstream_heads, input_heads, query_heads, key_heads):
    product = jnp.einsum(
        "htd,hjd->htj", upstream_heads, input_heads, preferred_element_type=jnp.float32
    )
    centre = jnp.sum(weights * product, axis=-1, keepdims=True)
    score_diff = (weights * (product - centre)).astype(jnp.bfloat16)
    scaling = 1.0 / math.sqrt(HD)
    query_out = (
        jnp.einsum("htj,hjd->htd", score_diff, key_heads, preferred_element_type=jnp.float32)
        * scaling
    ).astype(jnp.bfloat16)
    key_out = (
        jnp.einsum("htj,htd->hjd", score_diff, query_heads, preferred_element_type=jnp.float32)
        * scaling
    ).astype(jnp.bfloat16)
    return (from_heads(query_out), from_heads(key_out))


def dequantize(values, scales):
    value_heads = to_heads(values).astype(jnp.float32)
    scale_heads = scales.astype(jnp.float32).T[:, :, None]
    return (value_heads * scale_heads).astype(jnp.bfloat16)


def local(grad_in, loss_grad, queries, attn_keys, stored_input, block_scales):
    grad_first = grad_in[0]
    query_pair = queries[0]
    key_pair = attn_keys[0]
    is_last = lax.axis_index("section") == lax.axis_size("section") - 1
    query_first_heads = to_heads(query_pair[0])
    key_first_heads = to_heads(key_pair[0])
    grad_first_heads = to_heads(grad_first)
    weights_first = attention_weights(query_first_heads, key_first_heads)
    input_first = value_grad(weights_first, grad_first, grad_first_heads)
    received = passed_along(input_first, "section", -1)
    grad_second = jnp.where(is_last, loss_grad, received)
    grad_second_heads = to_heads(grad_second)
    query_second_heads = to_heads(query_pair[1])
    key_second_heads = to_heads(key_pair[1])
    weights_second = attention_weights(query_second_heads, key_second_heads)
    input_second = value_grad(weights_second, grad_second, grad_second_heads)
    columns, column_scales = (
        lax.all_to_all(stored_input[0], "tensor", split_axis=2, concat_axis=1, tiled=True),
        lax.all_to_all(block_scales[0], "tensor", split_axis=2, concat_axis=1, tiled=True),
    )
    inputs_first = dequantize(columns[0], column_scales[0])
    inputs_second = dequantize(columns[1], column_scales[1])
    query_first, key_first = score_grads(
        weights_first, grad_first_heads, inputs_first, query_first_heads, key_first_heads
    )
    query_second, key_second = score_grads(
        weights_second, grad_second_heads, inputs_second, query_second_heads, key_second_heads
    )
    grad_next = passed_along(input_second, "section", -1)
    query_grad = jnp.stack([query_first, query_second])
    key_grad = jnp.stack([key_first, key_second])
    return (grad_next[None], query_grad[None], key_grad[None])


def solution(mesh):
    return jax.shard_map(
        local,
        mesh=mesh,
        in_specs=(
            P("section", None, "tensor"),
            P(None, "tensor"),
            P("section", None, None, "tensor"),
            P("section", None, None, "tensor"),
            P("section", None, "tensor", None),
            P("section", None, "tensor", None),
        ),
        out_specs=(
            P("section", None, "tensor"),
            P("section", None, None, "tensor"),
            P("section", None, None, "tensor"),
        ),
        check_vma=False,
    )
```

profile of v0, /device:TPU:249, one launch (start us, length us, event | category | flops | bytes accessed | tf_op | source)
XLA Modules:
  0.0 87.2 jit_solution(11047999192089381704)
XLA Ops:
  0.6 0.6 iota_compare_fusion
  1.3 2.0 %fusion.51 = (bf16[1,1,256,768]{3,2,1,0:T(8,128)(2,1)}, bf16[1,1,256,768]{3,2,1,0:T(8,128)(2,1)S(1)}) fusion(bf16[1,2,256,768]{3,2,1,0:T(8,128)(2,1)} %param.8), kind=kLoop, calls=%fused_computation.60 | loop fusion | bytes 1572864 | tf_op jit(solution)/shard_map/slice | solution.py:85
  3.7 0.8 fusion.52
  5.1 1.6 %fusion.53 = (f32[6,256]{1,0:T(8,128)S(1)}, f32[6,256,256]{1,2,0:T(8,128)S(1)}) fusion(pred[256,256]{0,1:T(8,128)(4,1)} %iota_compare_fusion, bf16[256,6,128]{2,0,1:T(8,128)(2,1)S(1)} %copy.106, bf16[256,6,128]{2,0,1:T(8,128)(2,1)S(1)} %copy.104), kind=kOutput, calls=%fused_computation.62 | convolution fusion | flops 102236416 | bytes 2430976 | tf_op jit(solution)/shard_map/sub | solution.py:35
  6.7 0.4 fusion.19
  7.1 0.7 copy-done.7
  7.8 0.8 fusion.16
  8.7 2.6 %collective-permute-start = (bf16[256,768]{0,1:T(8,128)(2,1)}, bf16[256,768]{0,1:T(8,128)(2,1)}, u32[]{:S(2)}, u32[]{:S(2)}) collective-permute-start(bf16[256,768]{0,1:T(8,128)(2,1)} %fusion.16), channel_id=1, source_target_pairs={{8,0},{16,8},{24,16},{32,24},{40,32},{48,40},{56,48},{64,56},{72,6... | collective-permute-start | bytes 1179656 | tf_op jit(solution)/shard_map/ppermute | solution.py:13
  11.4 0.7 reshape.66
  12.1 5.2 %all-to-all-start.1 = ((bf16[8,2,192]{2,1,0:T(2,128)(2,1)}), bf16[8,2,192]{2,1,0:T(2,128)(2,1)S(1)}, u32[]{:S(2)}, u32[]{:S(2)}) async-start(bf16[8,2,192]{2,1,0:T(2,128)(2,1)} %reshape.66), calls=%async_computation.1 | async-start | bytes 16384 | tf_op jit(solution)/shard_map/all_to_all | solution.py:91
  17.3 5.1 %copy.115 = bf16[1,2,32,6144]{2,1,3,0:T(2,128)(2,1)} copy(bf16[1,2,32,6144]{3,2,1,0:T(8,128)(2,1)S(1)} %copy-done.14) | data formatting | bytes 1572864 | tf_op args[4]
  22.4 4.7 %bitcast_bitcast_fusion = bf16[6144,2,32]{2,1,0:T(2,128)(2,1)S(1)} fusion(bf16[1,2,32,6144]{2,1,3,0:T(2,128)(2,1)} %copy.115), kind=kLoop, calls=%fused_computation.64 | loop fusion | bytes 1572864
  27.1 1.9 %copy.109 = bf16[256,768]{0,1:T(8,128)(2,1)} copy(bf16[256,768]{1,0:T(8,128)(2,1)} %param.7) | data formatting | bytes 786432 | tf_op args[1]
  29.0 1.9 %copy.160 = bf16[1,1,256,768]{2,3,1,0:T(8,128)(2,1)} copy(bf16[1,1,256,768]{3,2,1,0:T(8,128)(2,1)} %get-tuple-element.14) | data formatting | bytes 786432
  30.9 1.9 %copy.111 = bf16[256,6,128]{2,0,1:T(8,128)(2,1)} copy(bf16[256,6,128]{0,2,1:T(8,128)(2,1)} %bitcast.150) | data formatting | bytes 786432 | tf_op jit(solution)/shard_map/reshape;squeeze | solution.py:18
  32.8 1.9 %copy.161 = bf16[1,1,256,768]{2,3,1,0:T(8,128)(2,1)} copy(bf16[1,1,256,768]{3,2,1,0:T(8,128)(2,1)} %get-tuple-element.16) | data formatting | bytes 786432
  34.7 1.9 %copy.113 = bf16[256,6,128]{2,0,1:T(8,128)(2,1)} copy(bf16[256,6,128]{0,2,1:T(8,128)(2,1)} %bitcast.152) | data formatting | bytes 786432 | tf_op jit(solution)/shard_map/reshape;squeeze | solution.py:18
  36.7 3.7 %reshape.64 = bf16[8,2,24576]{2,1,0:T(2,128)(2,1)} reshape(bf16[6144,2,32]{2,1,0:T(2,128)(2,1)S(1)} %bitcast_bitcast_fusion) | data formatting | bytes 1572864
  40.3 5.3 %all-to-all-start = ((bf16[8,2,24576]{2,1,0:T(2,128)(2,1)}), bf16[8,2,24576]{2,1,0:T(2,128)(2,1)}, u32[]{:S(2)}, u32[]{:S(2)}) async-start(bf16[8,2,24576]{2,1,0:T(2,128)(2,1)} %reshape.64), calls=%async_computation | async-start | bytes 1572864 | tf_op jit(solution)/shard_map/all_to_all | solution.py:90
  45.7 0.6 fusion.58
  46.3 0.3 copy-done.6
  46.6 1.3 %broadcast_select_fusion = bf16[256,768]{0,1:T(8,128)(2,1)S(1)} fusion(bf16[256,768]{0,1:T(8,128)(2,1)S(1)} %copy-done.6, bf16[256,768]{0,1:T(8,128)(2,1)} %collective-permute-done, pred[]{:T(512)S(6)} %eq.3), kind=kLoop, calls=%fused_computation.49 | loop fusion | flops 196608 | bytes 1179649 | tf_op jit(solution)/shard_map/jit(_where)/select_n | solution.py:83
  47.9 0.4 fusion.17
  48.3 0.3 copy-done.11
  48.8 4.6 %collective-permute-start.1 = (bf16[256,768]{0,1:T(8,128)(2,1)S(1)}, bf16[256,768]{0,1:T(8,128)(2,1)S(1)}, u32[]{:S(2)}, u32[]{:S(2)}) collective-permute-start(bf16[256,768]{0,1:T(8,128)(2,1)S(1)} %fusion.15), channel_id=1, source_target_pairs={{8,0},{16,8},{24,16},{32,24},{40,32},{48,40},{56,48},{64,56},{72,6... | collective-permute-start | bytes 1179656 | tf_op jit(solution)/shard_map/ppermute | solution.py:13
  53.6 0.8 copy.124
  54.4 0.8 copy.119
  55.2 12.1 %collective-permute-done.1 = bf16[256,768]{0,1:T(8,128)(2,1)S(1)} collective-permute-done((bf16[256,768]{0,1:T(8,128)(2,1)S(1)}, bf16[256,768]{0,1:T(8,128)(2,1)S(1)}, u32[]{:S(2)}, u32[]{:S(2)}) %collective-permute-start.1) | collective-permute-done | bytes 393248 | tf_op jit(solution)/shard_map/ppermute | solution.py:13
  67.3 0.9 %copy.137 = bf16[1,256,768]{2,1,0:T(8,128)(2,1)} copy(bf16[1,256,768]{1,2,0:T(8,128)(2,1)S(1)} %bitcast.163) | data formatting | bytes 786432
  68.2 3.2 %reshape.65 = bf16[6144,2,32]{2,1,0:T(2,128)(2,1)S(1)} reshape(bf16[8,2,24576]{2,1,0:T(2,128)(2,1)} %all-to-all-done) | data formatting | bytes 1572864
  71.4 4.9 %copy.116 = bf16[2,32,8,768]{3,1,2,0:T(8,128)(2,1)} copy(bf16[2,32,8,768]{1,0,3,2:T(2,128)(2,1)S(1)} %bitcast.145) | data formatting | bytes 1572864 | tf_op jit(solution)/shard_map/all_to_all | solution.py:90
  76.4 1.3 %slice_convert_fusion.1 = (f32[1,8,32,768]{3,2,1,0:T(8,128)S(1)}, f32[1,8,32,768]{3,2,1,0:T(8,128)S(1)}) fusion(bf16[2,8,32,768]{3,2,1,0:T(8,128)(2,1)} %bitcast.154), kind=kLoop, calls=%fused_computation.40 | loop fusion | flops 393216 | bytes 2359296 | tf_op jit(solution)/shard_map/convert_element_type | solution.py:67
  77.8 0.3 fusion.13
  78.2 0.5 copy-done.12
  78.7 0.6 copy-done.10
  79.3 0.4 multiply_reduce_fusion
  79.7 0.3 multiply_convert_fusion
  80.0 0.7 copy-done.2
  80.6 0.4 fusion.10
  81.2 0.3 fusion.12
  81.8 0.6 copy-done.15
  82.4 0.3 fusion.14
  82.8 1.1 %copy-done.8 = f32[6,256,256]{1,2,0:T(8,128)S(1)} copy-done((f32[6,256,256]{1,2,0:T(8,128)S(1)}, f32[6,256,256]{1,2,0:T(8,128)}, u32[]{:S(2)}) %copy-start.8) | copy-done | bytes 1572888
  83.9 0.4 fusion.4
  84.2 0.3 fusion.6
  84.5 0.4 fusion.9
  85.1 0.4 copy-done.1
  86.0 1.3 %maximum_bitcast_fusion = (bf16[1,2,256,768]{3,2,1,0:T(8,128)(2,1)}, bf16[1,2,256,768]{3,2,1,0:T(8,128)(2,1)}) fusion(bf16[1,256,768]{2,1,0:T(8,128)(2,1)S(1)} %copy.130, bf16[1,256,768]{2,1,0:T(8,128)(2,1)S(1)} %copy.129, bf16[1,256,768]{2,1,0:T(8,128)(2,1)S(1)} %copy.136, bf16[1,256,768]{2,1,0:T(8,128)(2,1)S(1)} %copy.135), kind=kLoop, calls=%fused_computation.27 | loop fusion | flops 786432 | bytes 3145728 | tf_op jit(solution)/shard_map/broadcast_in_dim | solution.py:104
  (62 shorter events, 2.7 us)
Async XLA Ops:
  1.3 2.4 %copy-start.13 = (bf16[1,2,256,768]{3,2,1,0:T(8,128)(2,1)S(1)}, bf16[1,2,256,768]{3,2,1,0:T(8,128)(2,1)}, u32[]{:S(2)}) copy-start(bf16[1,2,256,768]{3,2,1,0:T(8,128)(2,1)} %param.9) | copy-start | bytes 2359300
  3.7 1.2 %copy-start.17 = (bf16[1,256,768]{2,1,0:T(8,128)(2,1)S(1)}, bf16[1,256,768]{2,1,0:T(8,128)(2,1)}, u32[]{:S(2)}) copy-start(bf16[1,256,768]{2,1,0:T(8,128)(2,1)} %param.6) | copy-start | bytes 1179652
  4.7 2.0 %copy-start = (bf16[1,1,256,768]{2,3,1,0:T(8,128)(2,1)}, bf16[1,1,256,768]{2,3,1,0:T(8,128)(2,1)S(1)}, u32[]{:S(2)}) copy-start(bf16[1,1,256,768]{2,3,1,0:T(8,128)(2,1)S(1)} %copy.159) | copy-start | bytes 1179652
  5.1 2.0 %copy-start.4 = (bf16[1,256,768]{1,2,0:T(8,128)(2,1)}, bf16[1,256,768]{1,2,0:T(8,128)(2,1)S(1)}, u32[]{:S(2)}) copy-start(bf16[1,256,768]{1,2,0:T(8,128)(2,1)S(1)} %copy.102) | copy-start | bytes 1179652
  6.7 1.2 %copy-start.7 = (f32[6,256,256]{1,2,0:T(8,128)}, f32[6,256,256]{1,2,0:T(8,128)S(1)}, u32[]{:S(2)}) copy-start(f32[6,256,256]{1,2,0:T(8,128)S(1)} %get-tuple-element.21) | copy-start | bytes 4718596
  7.8 3.4 %copy-start.21 = (bf16[1,2,32,48]{3,2,1,0:T(8,128)(2,1)S(1)}, bf16[1,2,32,48]{3,2,1,0:T(8,128)(2,1)}, u32[]{:S(2)}) copy-start(bf16[1,2,32,48]{3,2,1,0:T(8,128)(2,1)} %param.11) | copy-start | bytes 18436
  7.8 9.4 %copy-start.14 = (bf16[1,2,32,6144]{3,2,1,0:T(8,128)(2,1)S(1)}, bf16[1,2,32,6144]{3,2,1,0:T(8,128)(2,1)}, u32[]{:S(2)}) copy-start(bf16[1,2,32,6144]{3,2,1,0:T(8,128)(2,1)} %param.10) | copy-start | bytes 2359300
  8.7 37.7 %collective-permute-start = (bf16[256,768]{0,1:T(8,128)(2,1)}, bf16[256,768]{0,1:T(8,128)(2,1)}, u32[]{:S(2)}, u32[]{:S(2)}) collective-permute-start(bf16[256,768]{0,1:T(8,128)(2,1)} %fusion.16), channel_id=1, source_target_pairs={{8,0},{16,8},{24,16},{32,24},{40,32},{48,40},{56,48},{64,56},{72,6... | collective-permute-start | bytes 1179656 | tf_op jit(solution)/shard_map/ppermute | solution.py:13
  12.1 28.3 %all-to-all-start.1 = ((bf16[8,2,192]{2,1,0:T(2,128)(2,1)}), bf16[8,2,192]{2,1,0:T(2,128)(2,1)S(1)}, u32[]{:S(2)}, u32[]{:S(2)}) async-start(bf16[8,2,192]{2,1,0:T(2,128)(2,1)} %reshape.66), calls=%async_computation.1 | async-start | bytes 16384 | tf_op jit(solution)/shard_map/all_to_all | solution.py:91
  40.3 5.3 %copy-start.18 = (bf16[256,6,128]{2,0,1:T(8,128)(2,1)S(1)}, bf16[256,6,128]{2,0,1:T(8,128)(2,1)}, u32[]{:S(2)}) copy-start(bf16[256,6,128]{2,0,1:T(8,128)(2,1)} %copy.111) | copy-start | bytes 1179652
  40.3 5.3 %copy-start.19 = (bf16[256,6,128]{2,0,1:T(8,128)(2,1)S(1)}, bf16[256,6,128]{2,0,1:T(8,128)(2,1)}, u32[]{:S(2)}) copy-start(bf16[256,6,128]{2,0,1:T(8,128)(2,1)} %copy.113) | copy-start | bytes 1179652
  40.3 5.3 %copy-start.20 = (pred[256,256]{0,1:T(8,128)(4,1)S(1)}, pred[256,256]{0,1:T(8,128)(4,1)}, u32[]{:S(2)}) copy-start(pred[256,256]{0,1:T(8,128)(4,1)} %iota_compare_fusion) | copy-start | bytes 196612
  40.3 27.9 %all-to-all-start = ((bf16[8,2,24576]{2,1,0:T(2,128)(2,1)}), bf16[8,2,24576]{2,1,0:T(2,128)(2,1)}, u32[]{:S(2)}, u32[]{:S(2)}) async-start(bf16[8,2,24576]{2,1,0:T(2,128)(2,1)} %reshape.64), calls=%async_computation | async-start | bytes 1572864 | tf_op jit(solution)/shard_map/all_to_all | solution.py:90
  45.6 1.0 %copy-start.6 = (bf16[256,768]{0,1:T(8,128)(2,1)S(1)}, bf16[256,768]{0,1:T(8,128)(2,1)}, u32[]{:S(2)}) copy-start(bf16[256,768]{0,1:T(8,128)(2,1)} %copy.109) | copy-start | bytes 1179652
  46.3 2.0 %copy-start.9 = (f32[6,256,256]{1,2,0:T(8,128)}, f32[6,256,256]{1,2,0:T(8,128)S(1)}, u32[]{:S(2)}) copy-start(f32[6,256,256]{1,2,0:T(8,128)S(1)} %get-tuple-element.23) | copy-start | bytes 4718596
  46.3 2.0 %copy-start.22 = (f32[6,256]{1,0:T(8,128)}, f32[6,256]{1,0:T(8,128)S(1)}, u32[]{:S(2)}) copy-start(f32[6,256]{1,0:T(8,128)S(1)} %get-tuple-element.22) | copy-start | bytes 18436
  47.9 0.8 copy-start.11
  48.8 18.5 %collective-permute-start.1 = (bf16[256,768]{0,1:T(8,128)(2,1)S(1)}, bf16[256,768]{0,1:T(8,128)(2,1)S(1)}, u32[]{:S(2)}, u32[]{:S(2)}) collective-permute-start(bf16[256,768]{0,1:T(8,128)(2,1)S(1)} %fusion.15), channel_id=1, source_target_pairs={{8,0},{16,8},{24,16},{32,24},{40,32},{48,40},{56,48},{64,56},{72,6... | collective-permute-start | bytes 1179656 | tf_op jit(solution)/shard_map/ppermute | solution.py:13
  76.4 1.5 %copy-start.16 = (f32[6,256]{0,1:T(8,128)S(1)}, f32[6,256]{0,1:T(8,128)}, u32[]{:S(2)}) copy-start(f32[6,256]{0,1:T(8,128)} %copy.124) | copy-start | bytes 18436
  77.7 1.0 %copy-start.12 = (bf16[256,768]{0,1:T(8,128)(2,1)S(1)}, bf16[256,768]{0,1:T(8,128)(2,1)}, u32[]{:S(2)}) copy-start(bf16[256,768]{0,1:T(8,128)(2,1)} %copy-done.11) | copy-start | bytes 1179652
  77.7 1.0 %copy-start.23 = (f32[6,256]{1,0:T(8,128)S(1)}, f32[6,256]{1,0:T(8,128)}, u32[]{:S(2)}) copy-start(f32[6,256]{1,0:T(8,128)} %copy-done.22) | copy-start | bytes 18436
  77.8 1.4 %copy-start.10 = (f32[6,256,256]{1,2,0:T(8,128)S(1)}, f32[6,256,256]{1,2,0:T(8,128)}, u32[]{:S(2)}) copy-start(f32[6,256,256]{1,2,0:T(8,128)} %copy-done.9) | copy-start | bytes 4718596
  79.6 1.0 %copy-start.2 = (bf16[1,1,256,768]{2,3,1,0:T(8,128)(2,1)S(1)}, bf16[1,1,256,768]{2,3,1,0:T(8,128)(2,1)}, u32[]{:S(2)}) copy-start(bf16[1,1,256,768]{2,3,1,0:T(8,128)(2,1)} %copy.160) | copy-start | bytes 1179652
  79.9 1.3 %copy-start.3 = (bf16[1,1,256,768]{2,3,1,0:T(8,128)(2,1)S(1)}, bf16[1,1,256,768]{2,3,1,0:T(8,128)(2,1)}, u32[]{:S(2)}) copy-start(bf16[1,1,256,768]{2,3,1,0:T(8,128)(2,1)} %copy.161) | copy-start | bytes 1179652
  81.5 0.9 %copy-start.15 = (f32[6,256]{0,1:T(8,128)S(1)}, f32[6,256]{0,1:T(8,128)}, u32[]{:S(2)}) copy-start(f32[6,256]{0,1:T(8,128)} %copy.119) | copy-start | bytes 18436
  81.7 1.1 %copy-start.5 = (bf16[1,256,768]{1,2,0:T(8,128)(2,1)S(1)}, bf16[1,256,768]{1,2,0:T(8,128)(2,1)}, u32[]{:S(2)}) copy-start(bf16[1,256,768]{1,2,0:T(8,128)(2,1)} %copy-done.4) | copy-start | bytes 1179652
  82.4 1.4 %copy-start.8 = (f32[6,256,256]{1,2,0:T(8,128)S(1)}, f32[6,256,256]{1,2,0:T(8,128)}, u32[]{:S(2)}) copy-start(f32[6,256,256]{1,2,0:T(8,128)} %copy-done.7) | copy-start | bytes 4718596
  84.5 1.0 %copy-start.1 = (bf16[1,1,256,768]{2,3,1,0:T(8,128)(2,1)S(1)}, bf16[1,1,256,768]{2,3,1,0:T(8,128)(2,1)}, u32[]{:S(2)}) copy-start(bf16[1,1,256,768]{2,3,1,0:T(8,128)(2,1)} %copy-done) | copy-start | bytes 1179652
where the time goes:
time: 88.1 us; the launch traced here: 87.2 us
  local copies, waits for them, and re-layouts  44.7 us (51%)
  starting transfers between devices  17.7 us (20%)
  waiting for transfers between devices  12.1 us (14%)
  other arithmetic  6.65 us (8%)
  matrix products  5.05 us (6%)
  between operations  1.09 us (1%)
    unnamed x63, local copies, waits for them, and re-layouts  30 us
    ppermute x2, waiting for transfers between devices, passed_along(): lax.ppermute(value, axis, [(source, source + steps) for source in range(l...  12.1 us
    ppermute x2, starting transfers between devices, passed_along(): lax.ppermute(value, axis, [(source, source + steps) for source in range(l...  7.17 us
    all_to_all x1, starting transfers between devices, local(): lax.all_to_all(stored_input[0], 'tensor', split_axis=2, concat_axis=1, ti...  5.29 us
    all_to_all x1, starting transfers between devices, local(): lax.all_to_all(block_scales[0], 'tensor', split_axis=2, concat_axis=1, ti...  5.2 us
    all_to_all x1, local copies, waits for them, and re-layouts, local(): lax.all_to_all(stored_input[0], 'tensor', split_axis=2, concat_axis=1, ti...  4.92 us
    another operation x4, local copies, waits for them, and re-layouts, to_heads(): return flat.reshape(tokens, width // HD, HD).transpose(1, 0, 2)  4.28 us
    sub x2, matrix products, attention_weights(): scores = scores - jnp.max(scores, axis=-1, keepdims=True)  2.21 us
  transfers between devices with their start and end apart: 4, of which 1 were waited for; matrix products, arithmetic and copies ran while one was open for 33% of the time, Pallas kernels for 0%

commit v1 on v0

--- a/solution.py
+++ b/solution.py
@@ -87,7 +87,15 @@
     weights_second = attention_weights(query_second_heads, key_second_heads)
     input_second = value_grad(weights_second, grad_second, grad_second_heads)
     columns, column_scales = (
-        lax.all_to_all(stored_input[0], "tensor", split_axis=2, concat_axis=1, tiled=True),
+        jnp.concatenate(
+            lax.all_to_all(
+                jnp.stack(jnp.split(stored_input[0], lax.axis_size("tensor"), axis=2)),
+                "tensor",
+                0,
+                0,
+            ),
+            axis=1,
+        ),
         lax.all_to_all(block_scales[0], "tensor", split_axis=2, concat_axis=1, tiled=True),
     )
     inputs_first = dequantize(columns[0], column_scales[0])

time: 88.1 us -> 68.6 us (0.78)
  the two profiles are of different devices: /device:TPU:249 before, /device:TPU:1 now
where the time goes in v1:
time: 68.6 us; the launch traced here: 67.9 us
  starting transfers between devices  19.5 us (28%)
  local copies, waits for them, and re-layouts  19.2 us (28%)
  matrix products  11.1 us (16%)
  waiting for transfers between devices  11.1 us (16%)
  other arithmetic  6.16 us (9%)
  between operations  0.98 us (1%)
    ppermute x2, waiting for transfers between devices, passed_along(): lax.ppermute(value, axis, [(source, source + steps) for source in range(l...  11.1 us
    unnamed x48, local copies, waits for them, and re-layouts  10.3 us
    ppermute x2, starting transfers between devices, passed_along(): lax.ppermute(value, axis, [(source, source + steps) for source in range(l...  8.24 us
    all_to_all x1, starting transfers between devices, local(): lax.all_to_all(block_scales[0], 'tensor', split_axis=2, concat_axis=1, ti...  5.86 us
    all_to_all x1, starting transfers between devices, local(): lax.all_to_all(jnp.stack(jnp.split(stored_input[0], lax.axis_size('tensor...  5.36 us
    sub x2, matrix products, attention_weights(): scores = scores - jnp.max(scores, axis=-1, keepdims=True)  5.13 us
    dot_general x2, matrix products, value_grad(): jnp.einsum('htj,htd->hjd', rounded, upstream_heads, preferred_element_typ...  2.36 us
    another operation x4, local copies, waits for them, and re-layouts, to_heads(): return flat.reshape(tokens, width // HD, HD).transpose(1, 0, 2)  2.28 us
  transfers between devices with their start and end apart: 4, of which 1 were waited for; matrix products, arithmetic and copies ran while one was open for 32% of the time, Pallas kernels for 0%

profile of v1, /device:TPU:1, one launch (start us, length us, event | category | flops | bytes accessed | tf_op | source)
XLA Modules:
  0.0 67.9 jit_solution(8091195314730275101)
XLA Ops:
  0.6 0.8 %copy.114 = bf16[1,2,32,48]{2,1,3,0:T(2,128)(2,1)S(1)} copy(bf16[1,2,32,48]{3,2,1,0:T(8,128)(2,1)} %param.11) | data formatting | bytes 12288 | tf_op args[5]
  1.5 0.7 %reshape.69 = bf16[8,2,192]{2,1,0:T(2,128)(2,1)} reshape(bf16[48,2,32]{2,1,0:T(2,128)(2,1)S(1)} %bitcast_bitcast_fusion) | data formatting | bytes 12288
  2.2 5.9 %all-to-all-start.1 = ((bf16[8,2,192]{2,1,0:T(2,128)(2,1)}), bf16[8,2,192]{2,1,0:T(2,128)(2,1)S(1)}, u32[]{:S(2)}, u32[]{:S(2)}) async-start(bf16[8,2,192]{2,1,0:T(2,128)(2,1)} %reshape.69), calls=%async_computation.1 | async-start | bytes 16384 | tf_op jit(solution)/shard_map/all_to_all | solution.py:99
  8.0 0.7 iota_compare_fusion
  8.7 1.2 %fusion.59 = (bf16[1,1,256,768]{3,2,1,0:T(8,128)(2,1)S(1)}, bf16[1,1,256,768]{3,2,1,0:T(8,128)(2,1)S(1)}) fusion(bf16[1,2,256,768]{3,2,1,0:T(8,128)(2,1)} %param.8), kind=kLoop, calls=%fused_computation.76 | loop fusion | bytes 1572864 | tf_op jit(solution)/shard_map/slice | solution.py:85
  10.1 0.9 %copy.103 = bf16[256,6,128]{2,0,1:T(8,128)(2,1)} copy(bf16[256,6,128]{0,2,1:T(8,128)(2,1)S(1)} %bitcast.176) | data formatting | bytes 786432 | tf_op jit(solution)/shard_map/reshape;squeeze | solution.py:18
  11.2 0.9 %copy.105 = bf16[256,6,128]{2,0,1:T(8,128)(2,1)} copy(bf16[256,6,128]{0,2,1:T(8,128)(2,1)S(1)} %bitcast.178) | data formatting | bytes 786432 | tf_op jit(solution)/shard_map/reshape;squeeze | solution.py:18
  12.3 1.9 %fusion.61 = (f32[6,256]{1,0:T(8,128)S(1)}, f32[6,256,256]{1,2,0:T(8,128)S(1)}) fusion(pred[256,256]{0,1:T(8,128)(4,1)} %iota_compare_fusion, bf16[256,6,128]{2,0,1:T(8,128)(2,1)} %copy.105, bf16[256,6,128]{2,0,1:T(8,128)(2,1)} %copy.103), kind=kOutput, calls=%fused_computation.78 | convolution fusion | flops 102236416 | bytes 2430976 | tf_op jit(solution)/shard_map/sub | solution.py:35
  14.3 0.4 fusion.19
  14.7 0.8 %fusion.16 = bf16[256,768]{0,1:T(8,128)(2,1)} fusion(f32[6,256,128]{1,2,0:T(8,128)S(1)} %fusion.19, bf16[1,256,768]{1,2,0:T(8,128)(2,1)S(1)} %copy.101), kind=kLoop, calls=%fused_computation.32 | loop fusion | flops 589824 | bytes 1572864 | tf_op jit(solution)/shard_map/convert_element_type | solution.py:45
  15.5 6.3 %collective-permute-start = (bf16[256,768]{0,1:T(8,128)(2,1)}, bf16[256,768]{0,1:T(8,128)(2,1)}, u32[]{:S(2)}, u32[]{:S(2)}) collective-permute-start(bf16[256,768]{0,1:T(8,128)(2,1)} %fusion.16), channel_id=1, source_target_pairs={{8,0},{16,8},{24,16},{32,24},{40,32},{48,40},{56,48},{64,56},{72,6... | collective-permute-start | bytes 1179656 | tf_op jit(solution)/shard_map/ppermute | solution.py:13
  21.9 0.6 fusion.36
  22.5 0.6 fusion.35
  23.2 0.6 fusion.34
  23.8 0.6 fusion.33
  24.5 0.6 fusion.32
  25.1 0.6 fusion.31
  25.8 0.6 fusion.30
  26.4 0.6 fusion.29
  27.4 0.2 copy.110
  27.8 0.2 copy.112
  28.1 5.4 %all-to-all-start = ((bf16[8,2,32,768]{3,2,1,0:T(8,128)(2,1)}), bf16[8,2,32,768]{3,2,1,0:T(8,128)(2,1)S(1)}, u32[]{:S(2)}, u32[]{:S(2)}) async-start(bf16[8,2,32,768]{3,2,1,0:T(8,128)(2,1)} %fusion.29), calls=%async_computation | async-start | bytes 1572864 | tf_op jit(solution)/shard_map/all_to_all | solution.py:91
  33.4 3.2 %fusion.66 = (f32[6,256]{1,0:T(8,128)}, f32[6,256,256]{1,2,0:T(8,128)}) fusion(pred[256,256]{0,1:T(8,128)(4,1)} %iota_compare_fusion, bf16[256,6,128]{2,0,1:T(8,128)(2,1)S(1)} %copy.112, bf16[256,6,128]{2,0,1:T(8,128)(2,1)S(1)} %copy.110), kind=kOutput, calls=%fused_computation.79 | convolution fusion | flops 102236416 | bytes 2430976 | tf_op jit(solution)/shard_map/sub | solution.py:35
  36.7 1.0 %broadcast_select_fusion = bf16[256,768]{0,1:T(8,128)(2,1)S(1)} fusion(bf16[256,768]{0,1:T(8,128)(2,1)S(1)} %copy.108, bf16[256,768]{0,1:T(8,128)(2,1)} %collective-permute-done, pred[]{:T(512)S(6)} %eq.3), kind=kLoop, calls=%fused_computation.49 | loop fusion | flops 196608 | bytes 1179649 | tf_op jit(solution)/shard_map/jit(_where)/select_n | solution.py:83
  37.7 2.0 %fusion.17 = f32[6,256,128]{1,2,0:T(8,128)S(1)} fusion(bf16[6,256,128]{1,2,0:T(8,128)(2,1)S(1)} %bitcast.191, f32[6,256,256]{1,2,0:T(8,128)} %get-tuple-element.23, f32[6,256]{1,0:T(8,128)} %get-tuple-element.22), kind=kOutput, calls=%fused_computation.33 | convolution fusion | flops 101449728 | bytes 2758656 | tf_op jit(solution)/shard_map/htj,htd->hjd/dot_general | solution.py:42
  39.8 1.9 %collective-permute-start.1 = (bf16[256,768]{0,1:T(8,128)(2,1)S(1)}, bf16[256,768]{0,1:T(8,128)(2,1)S(1)}, u32[]{:S(2)}, u32[]{:S(2)}) collective-permute-start(bf16[256,768]{0,1:T(8,128)(2,1)S(1)} %fusion.15), channel_id=1, source_target_pairs={{8,0},{16,8},{24,16},{32,24},{40,32},{48,40},{56,48},{64,56},{72,6... | collective-permute-start | bytes 1179656 | tf_op jit(solution)/shard_map/ppermute | solution.py:13
  42.1 0.8 %copy.121 = f32[6,256]{0,1:T(8,128)} copy(f32[6,256]{1,0:T(8,128)S(1)} %bitcast.205) | data formatting | bytes 12288 | tf_op jit(solution)/shard_map/transpose | solution.py:68
  42.9 11.1 %collective-permute-done.1 = bf16[256,768]{0,1:T(8,128)(2,1)S(1)} collective-permute-done((bf16[256,768]{0,1:T(8,128)(2,1)S(1)}, bf16[256,768]{0,1:T(8,128)(2,1)S(1)}, u32[]{:S(2)}, u32[]{:S(2)}) %collective-permute-start.1) | collective-permute-done | bytes 393248 | tf_op jit(solution)/shard_map/ppermute | solution.py:13
  54.0 0.9 %copy.134 = bf16[1,256,768]{2,1,0:T(8,128)(2,1)} copy(bf16[1,256,768]{1,2,0:T(8,128)(2,1)S(1)} %bitcast.201) | data formatting | bytes 786432
  54.9 1.0 %slice_convert_fusion.1 = (f32[1,8,32,768]{3,2,0,1:T(8,128)}, f32[1,8,32,768]{3,2,0,1:T(8,128)S(1)}) fusion(bf16[2,8,32,768]{3,2,0,1:T(8,128)(2,1)S(1)} %bitcast.184), kind=kLoop, calls=%fused_computation.40 | loop fusion | flops 393216 | bytes 2359296 | tf_op jit(solution)/shard_map/convert_element_type | solution.py:67
  55.9 1.3 %reshape.65 = f32[256,6,128]{2,1,0:T(8,128)S(1)} reshape(f32[1,8,32,768]{3,2,0,1:T(8,128)} %get-tuple-element.12) | data formatting | bytes 1572864 | tf_op jit(solution)/shard_map/convert_element_type | solution.py:67
  57.2 0.3 fusion.14
  57.5 0.6 copy-done.3
  58.2 1.9 %fusion.4 = (f32[6,256]{1,0:T(8,128)S(1)}, f32[6,256,256]{2,1,0:T(8,128)S(1)}) fusion(f32[6,256,256]{1,2,0:T(8,128)} %copy-done.4, f32[6,256]{1,0:T(8,128)S(1)} %get-tuple-element.20, bf16[6,256,128]{1,2,0:T(8,128)(2,1)S(1)} %bitcast.186, bf16[6,256,128]{2,0,1:T(8,128)(2,1)S(1)} %fusion.14), kind=kOutput, calls=%fused_computation.6 | convolution fusion | flops 101841408 | bytes 3944448 | tf_op jit(solution)/shard_map/htd,hjd->htj/dot_general | solution.py:49
  60.1 0.3 fusion.6
  60.4 0.4 fusion.9
  60.8 0.9 %copy.132 = bf16[1,256,768]{2,1,0:T(8,128)(2,1)} copy(bf16[1,256,768]{1,2,0:T(8,128)(2,1)S(1)} %bitcast.189) | data formatting | bytes 786432 | tf_op jit(solution)/shard_map/stack;reshape | solution.py:111
  61.7 0.3 fusion.11
  62.0 0.9 %copy.126 = bf16[1,256,768]{2,1,0:T(8,128)(2,1)} copy(bf16[1,256,768]{1,2,0:T(8,128)(2,1)S(1)} %bitcast.187) | data formatting | bytes 786432 | tf_op jit(solution)/shard_map/stack;reshape | solution.py:110
  63.0 0.3 fusion.13
  63.4 0.5 copy-done.8
  63.9 0.6 copy-done.6
  64.5 0.4 multiply_reduce_fusion
  64.8 0.3 multiply_convert_fusion
  65.1 0.4 fusion.10
  65.7 0.3 fusion.12
  66.2 0.3 copy-done
  66.6 1.3 %maximum_bitcast_fusion = (bf16[1,2,256,768]{3,2,1,0:T(8,128)(2,1)}, bf16[1,2,256,768]{3,2,1,0:T(8,128)(2,1)}) fusion(bf16[1,256,768]{2,1,0:T(8,128)(2,1)S(1)} %copy.127, bf16[1,256,768]{2,1,0:T(8,128)(2,1)S(1)} %copy-done.1, bf16[1,256,768]{2,1,0:T(8,128)(2,1)S(1)} %copy.133, bf16[1,256,768]{2,1,0:T(8,128)(2,1)S(1)} %copy-done), kind=kLoop, calls=%fused_computation.27 | loop fusion | flops 786432 | bytes 3145728 | tf_op jit(solution)/shard_map/broadcast_in_dim | solution.py:112
  (47 shorter events, 2.2 us)
Async XLA Ops:
  2.2 25.9 %all-to-all-start.1 = ((bf16[8,2,192]{2,1,0:T(2,128)(2,1)}), bf16[8,2,192]{2,1,0:T(2,128)(2,1)S(1)}, u32[]{:S(2)}, u32[]{:S(2)}) async-start(bf16[8,2,192]{2,1,0:T(2,128)(2,1)} %reshape.69), calls=%async_computation.1 | async-start | bytes 16384 | tf_op jit(solution)/shard_map/all_to_all | solution.py:99
  8.7 2.3 %copy-start.10 = (bf16[1,2,256,768]{3,2,1,0:T(8,128)(2,1)S(1)}, bf16[1,2,256,768]{3,2,1,0:T(8,128)(2,1)}, u32[]{:S(2)}) copy-start(bf16[1,2,256,768]{3,2,1,0:T(8,128)(2,1)} %param.9) | copy-start | bytes 2359300
  11.0 1.2 %copy-start.12 = (bf16[1,256,768]{2,1,0:T(8,128)(2,1)S(1)}, bf16[1,256,768]{2,1,0:T(8,128)(2,1)}, u32[]{:S(2)}) copy-start(bf16[1,256,768]{2,1,0:T(8,128)(2,1)} %param.6) | copy-start | bytes 1179652
  12.3 2.3 %copy-start.2 = (bf16[1,256,768]{1,2,0:T(8,128)(2,1)}, bf16[1,256,768]{1,2,0:T(8,128)(2,1)S(1)}, u32[]{:S(2)}) copy-start(bf16[1,256,768]{1,2,0:T(8,128)(2,1)S(1)} %copy.101) | copy-start | bytes 1179652
  14.3 12.8 %copy-start.4 = (f32[6,256,256]{1,2,0:T(8,128)}, f32[6,256,256]{1,2,0:T(8,128)S(1)}, u32[]{:S(2)}) copy-start(f32[6,256,256]{1,2,0:T(8,128)S(1)} %get-tuple-element.21) | copy-start | bytes 4718596
  14.7 7.2 %copy-start.9 = (bf16[1,2,32,6144]{3,2,1,0:T(8,128)(2,1)S(1)}, bf16[1,2,32,6144]{3,2,1,0:T(8,128)(2,1)}, u32[]{:S(2)}) copy-start(bf16[1,2,32,6144]{3,2,1,0:T(8,128)(2,1)} %param.10) | copy-start | bytes 2359300
  15.5 11.5 %copy-start.13 = (bf16[256,768]{1,0:T(8,128)(2,1)S(1)}, bf16[256,768]{1,0:T(8,128)(2,1)}, u32[]{:S(2)}) copy-start(bf16[256,768]{1,0:T(8,128)(2,1)} %param.7) | copy-start | bytes 1179652
  15.5 21.1 %collective-permute-start = (bf16[256,768]{0,1:T(8,128)(2,1)}, bf16[256,768]{0,1:T(8,128)(2,1)}, u32[]{:S(2)}, u32[]{:S(2)}) collective-permute-start(bf16[256,768]{0,1:T(8,128)(2,1)} %fusion.16), channel_id=1, source_target_pairs={{8,0},{16,8},{24,16},{32,24},{40,32},{48,40},{56,48},{64,56},{72,6... | collective-permute-start | bytes 1179656 | tf_op jit(solution)/shard_map/ppermute | solution.py:13
  28.1 26.8 %all-to-all-start = ((bf16[8,2,32,768]{3,2,1,0:T(8,128)(2,1)}), bf16[8,2,32,768]{3,2,1,0:T(8,128)(2,1)S(1)}, u32[]{:S(2)}, u32[]{:S(2)}) async-start(bf16[8,2,32,768]{3,2,1,0:T(8,128)(2,1)} %fusion.29), calls=%async_computation | async-start | bytes 1572864 | tf_op jit(solution)/shard_map/all_to_all | solution.py:91
  37.7 2.0 %copy-start.7 = (bf16[256,768]{0,1:T(8,128)(2,1)}, bf16[256,768]{0,1:T(8,128)(2,1)S(1)}, u32[]{:S(2)}) copy-start(bf16[256,768]{0,1:T(8,128)(2,1)S(1)} %broadcast_select_fusion) | copy-start | bytes 1179652
  39.8 14.2 %collective-permute-start.1 = (bf16[256,768]{0,1:T(8,128)(2,1)S(1)}, bf16[256,768]{0,1:T(8,128)(2,1)S(1)}, u32[]{:S(2)}, u32[]{:S(2)}) collective-permute-start(bf16[256,768]{0,1:T(8,128)(2,1)S(1)} %fusion.15), channel_id=1, source_target_pairs={{8,0},{16,8},{24,16},{32,24},{40,32},{48,40},{56,48},{64,56},{72,6... | collective-permute-start | bytes 1179656 | tf_op jit(solution)/shard_map/ppermute | solution.py:13
  57.2 1.0 %copy-start.3 = (bf16[1,256,768]{1,2,0:T(8,128)(2,1)S(1)}, bf16[1,256,768]{1,2,0:T(8,128)(2,1)}, u32[]{:S(2)}) copy-start(bf16[1,256,768]{1,2,0:T(8,128)(2,1)} %copy-done.2) | copy-start | bytes 1179652
  58.2 1.9 %copy-start.5 = (f32[6,256,256]{1,2,0:T(8,128)S(1)}, f32[6,256,256]{1,2,0:T(8,128)}, u32[]{:S(2)}) copy-start(f32[6,256,256]{1,2,0:T(8,128)} %copy-done.4) | copy-start | bytes 4718596
  62.0 1.1 %copy-start.11 = (f32[6,256]{0,1:T(8,128)S(1)}, f32[6,256]{0,1:T(8,128)}, u32[]{:S(2)}) copy-start(f32[6,256]{0,1:T(8,128)} %copy.121) | copy-start | bytes 18436
  62.9 1.0 %copy-start.8 = (bf16[256,768]{0,1:T(8,128)(2,1)S(1)}, bf16[256,768]{0,1:T(8,128)(2,1)}, u32[]{:S(2)}) copy-start(bf16[256,768]{0,1:T(8,128)(2,1)} %copy-done.7) | copy-start | bytes 1179652
  62.9 1.0 %copy-start.14 = (f32[6,256]{1,0:T(8,128)S(1)}, f32[6,256]{1,0:T(8,128)}, u32[]{:S(2)}) copy-start(f32[6,256]{1,0:T(8,128)} %get-tuple-element.22) | copy-start | bytes 18436
  63.0 1.4 %copy-start.6 = (f32[6,256,256]{1,2,0:T(8,128)S(1)}, f32[6,256,256]{1,2,0:T(8,128)}, u32[]{:S(2)}) copy-start(f32[6,256,256]{1,2,0:T(8,128)} %get-tuple-element.23) | copy-start | bytes 4718596
  65.5 1.0 %copy-start = (bf16[1,256,768]{2,1,0:T(8,128)(2,1)S(1)}, bf16[1,256,768]{2,1,0:T(8,128)(2,1)}, u32[]{:S(2)}) copy-start(bf16[1,256,768]{2,1,0:T(8,128)(2,1)} %copy.132) | copy-start | bytes 1179652
  65.5 1.1 %copy-start.1 = (bf16[1,256,768]{2,1,0:T(8,128)(2,1)S(1)}, bf16[1,256,768]{2,1,0:T(8,128)(2,1)}, u32[]{:S(2)}) copy-start(bf16[1,256,768]{2,1,0:T(8,128)(2,1)} %copy.126) | copy-start | bytes 1179652
